TPU v7x, 32 devices: a whole 2x2x4 slice. The times are simulated.
32 devices in a mesh: rcv: 4 (over z), src: 8 (over y, x, core).
Axes of the slice: x: 2, y: 2, z: 4, core: 2. Of those that a mesh axis runs over, the one named last changes fastest.
Arguments:
- reflection: bfloat16 [2, 16384, 16384], P(None, 'rcv', 'src'), may hold values from -6 to 6
- green: bfloat16 [2, 16384, 512], P(None, 'rcv', 'src'), may hold values from -0.046875 to 0.046875
- tile_mask: int32 [64, 64], replicated, may hold values from 0 to 1, as said below
- reference_index: int32 [512], P(('rcv', 'src')), may hold values from 0 to 511
Outputs:
- aligned: float32 [512, 2, 512], P(('rcv', 'src'))
Inputs may be any that keep to these rules, and one draw needn't show every extreme that they name: `tile_mask`: entries below the diagonal are 0.
All inputs are finite; a program needn't handle non-finite values.
Results may differ from a plain program's by a relative error of at most 0.02.
Values may be sent and summed in bfloat16 or wider, within the bound.
A program may use at most 256 MiB of HBM per device.

v0:
```python
import jax
import jax.numpy as jnp
from jax import lax
from jax.sharding import PartitionSpec as P

P_SIZE = 512
TILE = 256


def broadcast(block, axis, holder):
    block = jnp.where(lax.axis_index(axis) == holder, block, jnp.zeros_like(block))
    return lax.psum(block, axis)


def across(first, second, precision=None):
    return lax.dot_general(
        first,
        second,
        (((0,), (0,)), ((), ())),
        precision=precision,
        preferred_element_type=jnp.float32,
    )


def body(reflection, green, tile_mask, reference_index):
    rows_blk = reflection.shape[1]
    col_count = reflection.shape[2]
    rcv_index = lax.axis_index("rcv")
    src_index = lax.axis_index("src")
    green_block = lax.all_gather(green, "src", axis=2, tiled=True)
    src_per_rcv = lax.axis_size("src") // lax.axis_size("rcv")
    green_piece = lax.dynamic_slice_in_dim(
        green_block, src_index % src_per_rcv * col_count, col_count, 1
    )
    green_src = broadcast(green_piece, "rcv", src_index // src_per_rcv)
    row_tiles_count = rows_blk // TILE
    col_tiles_count = col_count // TILE
    tile_block = lax.dynamic_slice(
        tile_mask,
        (rcv_index * row_tiles_count, src_index * col_tiles_count),
        (row_tiles_count, col_tiles_count),
    )
    row_ids = rcv_index * row_tiles_count + jnp.arange(row_tiles_count)
    col_ids = src_index * col_tiles_count + jnp.arange(col_tiles_count)
    kept_tiles = tile_block == 1
    off_diag = kept_tiles & (row_ids[:, None] != col_ids[None, :])
    shaped = reflection.reshape(2, row_tiles_count, TILE, col_tiles_count, TILE)
    zero_value = jnp.zeros((), jnp.bfloat16)
    acquired = jnp.where(kept_tiles[None, :, None, :, None], shaped, zero_value).reshape(
        2, rows_blk, col_count
    )
    mirror_part = jnp.where(off_diag[None, :, None, :, None], shaped, zero_value).reshape(
        2, rows_blk, col_count
    )
    data_wide = jnp.concatenate([acquired[0], acquired[1], mirror_part[0], mirror_part[1]], axis=1)
    green_wide = jnp.concatenate([green_block[0], green_block[1]], axis=1)
    products = across(data_wide, green_wide)

    def quarter(row_slot, col_slot):
        return products[
            row_slot * col_count : (row_slot + 1) * col_count,
            col_slot * P_SIZE : (col_slot + 1) * P_SIZE,
        ]

    front_real = (quarter(0, 0) + quarter(1, 1)).astype(jnp.bfloat16)
    front_imag = (quarter(1, 0) - quarter(0, 1)).astype(jnp.bfloat16)
    back_real = (quarter(2, 0) - quarter(3, 1)).astype(jnp.bfloat16)
    back_imag = (quarter(3, 0) + quarter(2, 1)).astype(jnp.bfloat16)
    src_real = green_src[0]
    src_imag = green_src[1]
    green_stack = jnp.concatenate([src_real, src_imag], axis=0)
    mirror_left = jnp.concatenate(
        [
            jnp.concatenate([back_real, back_imag], axis=1),
            jnp.concatenate([back_imag, -back_real], axis=1),
        ],
        axis=0,
    )
    mirrored = across(green_stack, mirror_left)
    weights = jnp.concatenate(
        [
            jnp.concatenate([src_real, src_imag], axis=1),
            jnp.concatenate([-src_imag, src_real], axis=1),
        ],
        axis=0,
    )
    left_rows = jnp.concatenate([front_real, front_imag], axis=0)
    combined = across(left_rows, weights) + mirrored
    focal = lax.psum_scatter(combined, ("rcv", "src"), scatter_dimension=0, tiled=True)
    focal_real = focal[:, :P_SIZE]
    focal_imag = focal[:, P_SIZE:]
    chosen = jnp.arange(P_SIZE)[None, :] == reference_index[:, None]
    anchor_real = jnp.sum(jnp.where(chosen, focal_real, 0.0), axis=1)[:, None]
    anchor_imag = jnp.sum(jnp.where(chosen, focal_imag, 0.0), axis=1)[:, None]
    out_real = focal_real * anchor_real + focal_imag * anchor_imag
    out_imag = focal_imag * anchor_real - focal_real * anchor_imag
    return jnp.stack([out_real, out_imag], axis=1)


def solution(mesh):
    return jax.shard_map(
        body,
        mesh=mesh,
        in_specs=(P(None, "rcv", "src"), P(None, "rcv", "src"), P(), P(("rcv", "src"))),
        out_specs=P(("rcv", "src"), None, None),
        check_vma=False,
    )
```

profile of v0, /device:TPU:0, one launch (start us, length us, event | category | flops | bytes accessed | tf_op | source)
XLA Modules:
  0.0 491.1 jit_solution(2847651224598530955)
XLA Ops:
  6.5 0.0 all-gather.2.cloned.1.call-start
  6.5 0.7 all-gather.2.cloned.1.call-update
  7.3 0.0 all-reduce.2.cloned.1.call-start
  7.3 23.6 %copy.6 = bf16[1024,8,8,256]{3,2,1,0:T(8,128)(2,1)} copy(bf16[1024,8,8,256]{3,1,2,0:T(8,128)(2,1)} %bitcast.37) | data formatting | bytes 67108864
  30.9 0.8 compare_and_fusion
  31.7 32.3 %broadcast_select_fusion.1 = (bf16[2,16,256,8,256]{4,3,2,1,0:T(8,128)(2,1)}, bf16[2,16,256,8,256]{4,3,2,1,0:T(8,128)(2,1)}) fusion(bf16[2,16,256,8,256]{4,3,2,1,0:T(8,128)(2,1)} %bitcast.30, pred[16,8]{1,0:T(8,128)(4,1)S(1)} %get-tuple-element.10, pred[16,8]{1,0:T(8,128)(4,1)S(1)} %get-tuple-element.9), kind=kLoop, calls=%fused_computation.9 | loop fusion | flops 33554432 | bytes 100663552 | tf_op jit(solution)/shard_map/jit(_where)/select_n | solution.py:49
  64.0 38.8 %fusion.48 = (bf16[1,16,256,8,256]{4,3,2,1,0:T(8,128)(2,1)}, bf16[1,16,256,8,256]{4,3,2,1,0:T(8,128)(2,1)}, bf16[1,16,256,8,256]{4,3,2,1,0:T(8,128)(2,1)S(1)}, bf16[1,16,256,8,256]{4,3,2,1,0:T(8,128)(2,1)}) fusion(bf16[2,16,256,8,256]{4,3,2,1,0:T(8,128)(2,1)} %get-tuple-element.16, bf16[2,16,256,8,256]{4,3,2,1,0:T(8,128)(2,1)} %get-tuple-element.17), kind=kLoop, calls=%fused_computation.64 | loop fusion | bytes 134217728 | tf_op jit(solution)/shard_map/slice | solution.py:55
  102.8 16.3 %copy.7 = bf16[512,8,8,256]{3,1,2,0:T(8,128)(2,1)} copy(bf16[512,8,8,256]{3,2,1,0:T(8,128)(2,1)} %bitcast.36) | data formatting | bytes 33554432
  119.0 18.0 %copy.8 = bf16[512,8,8,256]{3,1,2,0:T(8,128)(2,1)} copy(bf16[512,8,8,256]{3,2,1,0:T(8,128)(2,1)} %bitcast.35) | data formatting | bytes 33554432
  137.1 0.0 slice-done
  137.1 0.0 slice-done.1
  137.1 0.0 slice-done.2
  137.1 9.8 %copy.9 = bf16[512,8,8,256]{3,1,2,0:T(8,128)(2,1)} copy(bf16[512,8,8,256]{3,2,1,0:T(8,128)(2,1)S(1)} %bitcast.34) | data formatting | bytes 33554432
  146.8 9.7 %copy.10 = bf16[512,8,8,256]{3,1,2,0:T(8,128)(2,1)} copy(bf16[512,8,8,256]{3,2,1,0:T(8,128)(2,1)S(1)} %bitcast.31) | data formatting | bytes 33554432
  156.6 5.6 %dynamic-slice_select_fusion = bf16[2,2048,512]{1,2,0:T(8,128)(2,1)} fusion(bf16[2,4096,512]{1,2,0:T(8,128)(2,1)} %all-gather.2.cloned.1.call-done, s32[]{:T(128)S(6)} %select_n.49, pred[]{:T(512)S(6)} %eq.26), kind=kLoop, calls=%fused_computation.45 | loop fusion | flops 2097152 | bytes 8388613 | tf_op jit(solution)/shard_map/jit(_where)/select_n | solution.py:11
  162.1 0.0 all-reduce.2.cloned.1.call-update
  162.1 0.2 reduce-scatter.2.cloned.1.call-start
  162.4 6.0 %slice_bitcast_fusion.1 = (bf16[4096,512]{0,1:T(8,128)(2,1)}, bf16[4096,512]{0,1:T(8,128)(2,1)}) fusion(bf16[2,4096,512]{1,2,0:T(8,128)(2,1)} %all-gather.2.cloned.1.call-done), kind=kLoop, calls=%fused_computation.38 | loop fusion | bytes 16777216 | tf_op jit(solution)/shard_map/squeeze | solution.py:56
  168.3 107.8 %fusion = f32[8192,1024]{0,1:T(8,128)} fusion(bf16[4096,2048]{1,0:T(8,128)(2,1)} %bitcast.41, bf16[4096,2048]{1,0:T(8,128)(2,1)} %bitcast.40, bf16[4096,2048]{1,0:T(8,128)(2,1)} %bitcast.39, bf16[4096,2048]{1,0:T(8,128)(2,1)} %bitcast.38, bf16[4096,512]{0,1:T(8,128)(2,1)} %get-tuple-element.21, bf16[4096,512]{0,1:T(8,128)(2,1)} %get-tuple-element.20), kind=kOutput, calls=%fused_computation | convolution fusion | flops 69004689408 | bytes 109051904 | tf_op jit(solution)/shard_map/dot_general | solution.py:16
  276.1 6.0 %fusion.46 = (bf16[2048,512]{0,1:T(8,128)(2,1)S(1)}, bf16[2048,512]{0,1:T(8,128)(2,1)}) fusion(f32[8192,1024]{0,1:T(8,128)} %fusion), kind=kLoop, calls=%fused_computation.63 | loop fusion | flops 3145728 | bytes 12582912 | tf_op jit(solution)/shard_map/neg | solution.py:75
  282.1 11.8 %fusion.27 = (bf16[2048,512]{0,1:T(8,128)(2,1)}, bf16[2048,512]{0,1:T(8,128)(2,1)}, bf16[2048,512]{0,1:T(8,128)(2,1)}) fusion(f32[8192,1024]{0,1:T(8,128)} %fusion), kind=kLoop, calls=%fused_computation.30 | loop fusion | flops 6291456 | bytes 31457280 | tf_op jit(solution)/shard_map/convert_element_type | solution.py:68
  293.9 25.8 %all-reduce.2.cloned.1.call-done = bf16[2,2048,512]{1,2,0:T(8,128)(2,1)} async-done(((bf16[2,2048,512]{1,2,0:T(8,128)(2,1)}), bf16[2,2048,512]{1,2,0:T(8,128)(2,1)}) %all-reduce.2.cloned.1.call-update) | async-done | bytes 4194320 | tf_op jit(solution)/shard_map/psum | solution.py:12
  319.8 4.9 %slice_bitcast_fusion.2 = (bf16[2048,512]{0,1:T(8,128)(2,1)}, bf16[2048,512]{0,1:T(8,128)(2,1)}) fusion(bf16[2,2048,512]{1,2,0:T(8,128)(2,1)} %all-reduce.2.cloned.1.call-done), kind=kLoop, calls=%fused_computation.46 | loop fusion | bytes 8388608 | tf_op jit(solution)/shard_map/squeeze | solution.py:70
  324.7 0.0 copy-done
  324.7 0.1 fusion.45
  324.8 10.1 %fusion.11 = f32[512,1024]{1,0:T(8,128)} fusion(bf16[2048,512]{0,1:T(8,128)(2,1)} %get-tuple-element.23, bf16[2048,512]{0,1:T(8,128)(2,1)S(1)} %fusion.45, bf16[2048,512]{0,1:T(8,128)(2,1)} %get-tuple-element.22, bf16[2048,512]{0,1:T(8,128)(2,1)} %get-tuple-element.12, bf16[2048,512]{0,1:T(8,128)(2,1)} %get-tuple-element.13), kind=kOutput, calls=%fused_computation.13 | convolution fusion | flops 4336910336 | bytes 12582912 | tf_op jit(solution)/shard_map/dot_general | solution.py:16
  334.9 9.9 %fusion.37 = f32[512,1024]{1,0:T(8,128)} fusion(f32[512,1024]{1,0:T(8,128)} %fusion.11, bf16[2048,512]{0,1:T(8,128)(2,1)S(1)} %get-tuple-element.7, bf16[2048,512]{0,1:T(8,128)(2,1)} %get-tuple-element.11, bf16[2048,512]{0,1:T(8,128)(2,1)S(1)} %copy-done.1, bf16[2048,512]{0,1:T(8,128)(2,1)} %get-tuple-element.22, bf16[2048,512]{0,1:T(8,128)(2,1)} %get-tuple-element.23), kind=kOutput, calls=%fused_computation.48 | convolution fusion | flops 4337434624 | bytes 14680064 | tf_op jit(solution)/shard_map/dot_general | solution.py:16
  344.9 0.0 reduce-scatter.2.cloned.1.call-update
  344.9 137.1 %reduce-scatter.2.cloned.1.call-done = f32[16,1024]{1,0:T(8,128)} async-done(((f32[512,1024]{1,0:T(8,128)}), f32[16,1024]{1,0:T(8,128)}) %reduce-scatter.2.cloned.1.call-update) | async-done | bytes 65552 | tf_op jit(solution)/shard_map/reduce_scatter | solution.py:89
  482.0 1.0 select_reduce_fusion.1
  483.0 0.9 add_bitcast_fusion
  483.8 0.7 copy.5
  (15 shorter events, 0.0 us)
Async XLA Ops:
  6.5 150.0 %all-gather.2.cloned.1.call-start = ((), (), s32[]{:S(2)}) async-start(), calls=%async_computation.1 | async-start | bytes 9437184 | tf_op jit(solution)/shard_map/all_gather | solution.py:30
  7.3 312.5 %all-reduce.2.cloned.1.call-start = ((), (), s32[]{:S(2)}) async-start(), calls=%async_computation.2 | async-start | bytes 8388608 | tf_op jit(solution)/shard_map/psum | solution.py:12
  119.0 18.0 %slice-start = ((s8[16777216]{0:T(1024)(128)(4,1)}), s8[4194304]{0:T(1024)(128)(4,1)S(1)}, s32[]{:S(2)}) async-start(s8[16777216]{0:T(1024)(128)(4,1)} %bitcast.32), calls=%async_computation.4 | async-start | bytes 8388608
  119.0 18.0 %slice-start.1 = ((s8[16777216]{0:T(1024)(128)(4,1)}), s8[4194304]{0:T(1024)(128)(4,1)S(1)}, s32[]{:S(2)}) async-start(s8[16777216]{0:T(1024)(128)(4,1)} %bitcast.32), calls=%async_computation.5 | async-start | bytes 8388608
  119.0 18.0 %slice-start.2 = ((s8[16777216]{0:T(1024)(128)(4,1)}), s8[4194304]{0:T(1024)(128)(4,1)S(1)}, s32[]{:S(2)}) async-start(s8[16777216]{0:T(1024)(128)(4,1)} %bitcast.32), calls=%async_computation.6 | async-start | bytes 8388608
  119.0 18.0 %slice-start.3 = ((s8[16777216]{0:T(1024)(128)(4,1)}), s8[4194304]{0:T(1024)(128)(4,1)S(1)}, s32[]{:S(2)}) async-start(s8[16777216]{0:T(1024)(128)(4,1)} %bitcast.32), calls=%async_computation.7 | async-start | bytes 8388608
  162.1 319.9 %reduce-scatter.2.cloned.1.call-start = ((), (), s32[]{:S(2)}) async-start(), calls=%async_computation.3 | async-start | bytes 2162688 | tf_op jit(solution)/shard_map/reduce_scatter | solution.py:89
  319.8 4.9 %copy-start = (bf16[2,2048,512]{1,2,0:T(8,128)(2,1)S(1)}, bf16[2,2048,512]{1,2,0:T(8,128)(2,1)}, u32[]{:S(2)}) copy-start(bf16[2,2048,512]{1,2,0:T(8,128)(2,1)} %all-reduce.2.cloned.1.call-done) | copy-start | bytes 12582916
  324.8 10.1 %copy-start.1 = (bf16[2048,512]{0,1:T(8,128)(2,1)S(1)}, bf16[2048,512]{0,1:T(8,128)(2,1)}, u32[]{:S(2)}) copy-start(bf16[2048,512]{0,1:T(8,128)(2,1)} %get-tuple-element.8) | copy-start | bytes 6291460
  334.9 147.1 %copy-start.2 = (s32[16]{0:T(128)S(1)}, s32[16]{0:T(128)}, u32[]{:S(2)}) copy-start(s32[16]{0:T(128)} %param.7) | copy-start | bytes 196
Sparse Core Ops, SparseCore 0:
  9.2 56.9 all-gather.1
  162.3 157.4 all-reduce.1
  345.0 136.9 reduce-scatter.1
where the time goes:
time: 491 us
  waiting for transfers between devices  164 us (33%)
  local copies, waits for them, and re-layouts  128 us (26%)
  matrix products  128 us (26%)
  other arithmetic  58.4 us (12%)
  between operations  13.2 us (3%)
    reduce_scatter x1, waiting for transfers between devices, body(): lax.psum_scatter(combined, ('rcv', 'src'), scatter_dimension=0, tiled=True)  137 us
    dot_general x3, matrix products, across(): lax.dot_general(first, second, (((0,), (0,)), ((), ())), precision=precis...  128 us
    unnamed x19, local copies, waits for them, and re-layouts  77.4 us
    slice x1, local copies, waits for them, and re-layouts, body(): acquired[0]  38.8 us
    select_n x1, other arithmetic, body(): jnp.where(kept_tiles[None, :, None, :, None], shaped, zero_value)  32.3 us
    psum x1, waiting for transfers between devices, broadcast(): return lax.psum(block, axis)  25.8 us
    convert_element_type x1, other arithmetic, body(): back_imag = (quarter(3, 0) + quarter(2, 1)).astype(jnp.bfloat16)  11.8 us
  transfers between devices with their start and end apart: 3, of which 2 were waited for; matrix products, arithmetic and copies ran while one was open for 57% of the time, Pallas kernels for 0%

commit v1 on v0

--- a/solution.py
+++ b/solution.py
@@ -7,9 +7,14 @@
 TILE = 256
 
 
+def perform_layers_all(local_array, axis_tag):
+    piece_now = jnp.sum(lax.all_gather(local_array, axis_tag), axis=0)
+    return piece_now
+
+
 def broadcast(block, axis, holder):
     block = jnp.where(lax.axis_index(axis) == holder, block, jnp.zeros_like(block))
-    return lax.psum(block, axis)
+    return perform_layers_all(block, axis)
 
 
 def across(first, second, precision=None):

time: 491 us -> 717 us (1.46)
  waiting for transfers between devices: 164 us -> 290 us
  local copies, waits for them, and re-layouts: 128 us -> 199 us
  other arithmetic: 58.4 us -> 82.5 us
    all_gather x0 -> x1, waiting for transfers between devices: none -> 154 us  [perform_layers_all(): piece_now = jnp.sum(lax.all_gather(local_array, axis_tag), axis=0)]
    unnamed x19 -> x22, local copies, waits for them, and re-layouts: 77.4 us -> 124 us
    psum x1 -> x0, waiting for transfers between devices: 25.8 us -> none  [broadcast(): return lax.psum(block, axis)]
    slice x0 -> x2, local copies, waits for them, and re-layouts: none -> 25.1 us  [the longest x1 20.6 us: body(): green_wide = jnp.concatenate([green_block[0], green_block[1]], axis=1)]
    reduce_sum x0 -> x1, other arithmetic: none -> 11.8 us  [perform_layers_all(): piece_now = jnp.sum(lax.all_gather(local_array, axis_tag), axis=0)]
    select_n x0 -> x1, local copies, waits for them, and re-layouts: none -> 11.1 us  [broadcast(): jnp.where(lax.axis_index(axis) == holder, block, jnp.zeros_like(block))]
    squeeze x2 -> x0, local copies, waits for them, and re-layouts: 10.9 us -> none  [the longest x1 5.96 us: body(): green_wide = jnp.concatenate([green_block[0], green_block[1]], axis=1)]
    dot_general x0 -> x1, other arithmetic: none -> 7.96 us  [across(): lax.dot_general(first, second, (((0,), (0,)), ((), ())), precision=precis...]
  transfers between devices with their start and end apart: 3 -> 3, of which waited for: 2 -> 2; matrix products, arithmetic and copies ran while one was open for 57% -> 40% of each run, Pallas kernels for 0% -> 0%
where the time goes in v1:
time: 717 us; the launch traced here: 715 us
  waiting for transfers between devices  290 us (40%)
  local copies, waits for them, and re-layouts  199 us (28%)
  matrix products  130 us (18%)
  other arithmetic  82.5 us (12%)
  between operations  13.2 us (2%)
    all_gather x1, waiting for transfers between devices, perform_layers_all(): piece_now = jnp.sum(lax.all_gather(local_array, axis_tag), axis=0)  154 us
    reduce_scatter x1, waiting for transfers between devices, body(): lax.psum_scatter(combined, ('rcv', 'src'), scatter_dimension=0, tiled=True)  137 us
    dot_general x3, matrix products, across(): lax.dot_general(first, second, (((0,), (0,)), ((), ())), precision=precis...  130 us
    unnamed x22, local copies, waits for them, and re-layouts  124 us
    slice x1, local copies, waits for them, and re-layouts, body(): acquired[0]  38.6 us
    select_n x1, other arithmetic, body(): jnp.where(kept_tiles[None, :, None, :, None], shaped, zero_value)  32.4 us
    slice x1, local copies, waits for them, and re-layouts, body(): green_wide = jnp.concatenate([green_block[0], green_block[1]], axis=1)  20.6 us
  transfers between devices with their start and end apart: 3, of which 2 were waited for; matrix products, arithmetic and copies ran while one was open for 40% of the time, Pallas kernels for 0%

profile of v1, /device:TPU:0, one launch (start us, length us, event | category | flops | bytes accessed | tf_op | source)
XLA Modules:
  0.0 715.3 jit_solution(13542532985357125101)
XLA Ops:
  6.5 3.3 copy.14
  9.9 0.0 all-gather.6.cloned.1.call-start
  9.9 23.3 %copy.25 = bf16[1024,8,8,256]{3,2,1,0:T(8,128)(2,1)} copy(bf16[1024,8,8,256]{3,1,2,0:T(8,128)(2,1)} %bitcast.34) | data formatting | bytes 67108864
  33.2 0.8 compare_and_fusion
  34.0 32.4 %broadcast_select_fusion.1 = (bf16[2,16,256,8,256]{4,3,2,1,0:T(8,128)(2,1)}, bf16[2,16,256,8,256]{4,3,2,1,0:T(8,128)(2,1)}) fusion(bf16[2,16,256,8,256]{4,3,2,1,0:T(8,128)(2,1)} %bitcast.27, pred[16,8]{1,0:T(8,128)(4,1)S(1)} %get-tuple-element.10, pred[16,8]{1,0:T(8,128)(4,1)S(1)} %get-tuple-element.9), kind=kLoop, calls=%fused_computation.9 | loop fusion | flops 33554432 | bytes 100663552 | tf_op jit(solution)/shard_map/jit(_where)/select_n | solution.py:54
  66.4 38.6 %fusion.47 = (bf16[1,16,256,8,256]{4,3,2,1,0:T(8,128)(2,1)}, bf16[1,16,256,8,256]{4,3,2,1,0:T(8,128)(2,1)}, bf16[1,16,256,8,256]{4,3,2,1,0:T(8,128)(2,1)S(1)}, bf16[1,16,256,8,256]{4,3,2,1,0:T(8,128)(2,1)}) fusion(bf16[2,16,256,8,256]{4,3,2,1,0:T(8,128)(2,1)} %get-tuple-element.16, bf16[2,16,256,8,256]{4,3,2,1,0:T(8,128)(2,1)} %get-tuple-element.17), kind=kLoop, calls=%fused_computation.60 | loop fusion | bytes 134217728 | tf_op jit(solution)/shard_map/slice | solution.py:60
  105.1 16.3 %copy.26 = bf16[512,8,8,256]{3,1,2,0:T(8,128)(2,1)} copy(bf16[512,8,8,256]{3,2,1,0:T(8,128)(2,1)} %bitcast.33) | data formatting | bytes 33554432
  121.3 18.0 %copy.27 = bf16[512,8,8,256]{3,1,2,0:T(8,128)(2,1)} copy(bf16[512,8,8,256]{3,2,1,0:T(8,128)(2,1)} %bitcast.32) | data formatting | bytes 33554432
  139.4 9.7 %copy.28 = bf16[512,8,8,256]{3,1,2,0:T(8,128)(2,1)} copy(bf16[512,8,8,256]{3,2,1,0:T(8,128)(2,1)S(1)} %bitcast.31) | data formatting | bytes 33554432
  149.1 9.7 %copy.29 = bf16[512,8,8,256]{3,1,2,0:T(8,128)(2,1)} copy(bf16[512,8,8,256]{3,2,1,0:T(8,128)(2,1)S(1)} %bitcast.28) | data formatting | bytes 33554432
  158.8 20.6 %fusion.49 = (bf16[1,4096,512]{1,0,2:T(2,128)(2,1)}, bf16[1,4096,512]{1,0,2:T(2,128)(2,1)}) fusion(bf16[2,4096,512]{1,0,2:T(2,128)(2,1)} %all-gather.4.cloned.1.call-done), kind=kLoop, calls=%fused_computation.62 | loop fusion | bytes 16777216 | tf_op jit(solution)/shard_map/slice | solution.py:61
  179.3 18.3 %copy.21 = bf16[1,4096,512]{2,1,0:T(8,128)(2,1)} copy(bf16[1,4096,512]{1,0,2:T(2,128)(2,1)} %get-tuple-element.20) | data formatting | bytes 8388608
  197.7 18.3 %copy.22 = bf16[1,4096,512]{2,1,0:T(8,128)(2,1)} copy(bf16[1,4096,512]{1,0,2:T(2,128)(2,1)} %get-tuple-element.21) | data formatting | bytes 8388608
  216.0 7.9 %broadcast_select_fusion.2 = bf16[2,2048,512]{1,0,2:T(2,128)(2,1)} fusion(pred[]{:T(512)S(6)} %eq.26, bf16[2,4096,512]{1,0,2:T(2,128)(2,1)} %all-gather.4.cloned.1.call-done, s32[]{:T(128)S(6)} %select_n.49), kind=kLoop, calls=%fused_computation.29 | loop fusion | flops 2097152 | bytes 8388613 | tf_op jit(solution)/shard_map/jit(_where)/select_n | solution.py:16
  223.9 11.1 %copy.17 = bf16[2,2048,512]{2,1,0:T(8,128)(2,1)} copy(bf16[2,2048,512]{1,0,2:T(2,128)(2,1)} %broadcast_select_fusion.2) | data formatting | bytes 8388608 | tf_op jit(solution)/shard_map/jit(_where)/select_n | solution.py:16
  235.1 0.2 reduce-scatter.2.cloned.1.call-start
  235.3 8.0 %fusion.57 = bf16[4096,1024]{1,0:T(8,128)(2,1)} fusion(bf16[4096,512]{1,0:T(8,128)(2,1)} %bitcast.41, bf16[4096,512]{1,0:T(8,128)(2,1)} %bitcast.40), kind=kLoop, calls=%fused_computation.10.clone.2 | loop fusion | flops 16777216 | bytes 16777216 | tf_op jit(solution)/shard_map/dot_general | solution.py:21
  243.3 109.7 %fusion = f32[8192,1024]{0,1:T(8,128)} fusion(bf16[4096,2048]{1,0:T(8,128)(2,1)} %bitcast.38, bf16[4096,2048]{1,0:T(8,128)(2,1)} %bitcast.37, bf16[4096,2048]{1,0:T(8,128)(2,1)} %bitcast.36, bf16[4096,2048]{1,0:T(8,128)(2,1)} %bitcast.35, bf16[4096,1024]{1,0:T(8,128)(2,1)} %fusion.57), kind=kOutput, calls=%fused_computation | convolution fusion | flops 68987912192 | bytes 109051904 | tf_op jit(solution)/shard_map/dot_general | solution.py:21
  353.0 6.6 fusion.45
  359.6 11.7 %fusion.27 = (bf16[2048,512]{0,1:T(8,128)(2,1)}, bf16[2048,512]{0,1:T(8,128)(2,1)}, bf16[2048,512]{0,1:T(8,128)(2,1)}) fusion(f32[8192,1024]{0,1:T(8,128)} %fusion), kind=kLoop, calls=%fused_computation.31 | loop fusion | flops 6291456 | bytes 31457280 | tf_op jit(solution)/shard_map/convert_element_type | solution.py:73
  371.3 153.7 %all-gather.6.cloned.1.call-done = bf16[8,2048,512]{2,1,0:T(8,128)(2,1)} async-done(((bf16[2,2048,512]{2,1,0:T(8,128)(2,1)}), bf16[8,2048,512]{2,1,0:T(8,128)(2,1)}) %all-gather.6.cloned.1.call-update) | async-done | bytes 16777232 | tf_op jit(solution)/shard_map/all_gather | solution.py:11
  525.0 11.8 %reduce_sum.30 = bf16[2,2048,512]{2,1,0:T(8,128)(2,1)} reduce(bf16[4,2,2048,512]{3,2,1,0:T(8,128)(2,1)} %bitcast.39, bf16[]{:T(256)} %constant.44.clone.1), dimensions={0}, to_apply=%region_0.1 | reduce | flops 6291456 | bytes 20971522 | tf_op jit(solution)/shard_map/reduce_sum | solution.py:11
  536.8 4.5 fusion.50
  541.3 2.9 copy.24
  544.2 1.5 bitcast_negate_fusion
  545.7 3.9 copy.23
  549.6 10.1 %fusion.11 = f32[512,1024]{1,0:T(8,128)} fusion(bf16[2048,512]{0,1:T(8,128)(2,1)} %bitcast.44, bf16[2048,512]{0,1:T(8,128)(2,1)} %bitcast_negate_fusion, bf16[2048,512]{0,1:T(8,128)(2,1)S(1)} %bitcast.42, bf16[2048,512]{0,1:T(8,128)(2,1)} %get-tuple-element.12, bf16[2048,512]{0,1:T(8,128)(2,1)} %get-tuple-element.13), kind=kOutput, calls=%fused_computation.13 | convolution fusion | flops 4336910336 | bytes 12582912 | tf_op jit(solution)/shard_map/dot_general | solution.py:21
  559.7 10.0 %fusion.37 = f32[512,1024]{1,0:T(8,128)} fusion(f32[512,1024]{1,0:T(8,128)} %fusion.11, bf16[2048,512]{0,1:T(8,128)(2,1)} %get-tuple-element.7, bf16[2048,512]{0,1:T(8,128)(2,1)} %get-tuple-element.11, bf16[2048,512]{0,1:T(8,128)(2,1)} %get-tuple-element.8, bf16[2048,512]{0,1:T(8,128)(2,1)S(1)} %bitcast.43, bf16[2048,512]{0,1:T(8,128)(2,1)S(1)} %bitcast.45), kind=kOutput, calls=%fused_computation.44 | convolution fusion | flops 4337434624 | bytes 14680064 | tf_op jit(solution)/shard_map/dot_general | solution.py:21
  569.7 136.6 %reduce-scatter.2.cloned.1.call-done = f32[16,1024]{1,0:T(8,128)} async-done(((f32[512,1024]{1,0:T(8,128)}), f32[16,1024]{1,0:T(8,128)}) %reduce-scatter.2.cloned.1.call-update) | async-done | bytes 65552 | tf_op jit(solution)/shard_map/reduce_scatter | solution.py:94
  706.3 1.0 select_reduce_fusion.1
  707.2 0.9 add_bitcast_fusion
  708.1 0.7 copy.19
  (21 shorter events, 0.1 us)
Async XLA Ops:
  6.5 152.2 %all-gather.4.cloned.1.call-start = ((), (), s32[]{:S(2)}) async-start(), calls=%async_computation.1 | async-start | bytes 9437184 | tf_op jit(solution)/shard_map/all_gather | solution.py:35
  9.9 515.1 %all-gather.6.cloned.1.call-start = ((), (), s32[]{:S(2)}) async-start(), calls=%async_computation.3 | async-start | bytes 20971520 | tf_op jit(solution)/shard_map/all_gather | solution.py:11
  121.3 18.0 %slice-start = ((s8[16777216]{0:T(1024)(128)(4,1)}), s8[4194304]{0:T(1024)(128)(4,1)S(1)}, s32[]{:S(2)}) async-start(s8[16777216]{0:T(1024)(128)(4,1)} %bitcast.29), calls=%async_computation.4 | async-start | bytes 8388608
  121.3 18.0 %slice-start.1 = ((s8[16777216]{0:T(1024)(128)(4,1)}), s8[4194304]{0:T(1024)(128)(4,1)S(1)}, s32[]{:S(2)}) async-start(s8[16777216]{0:T(1024)(128)(4,1)} %bitcast.29), calls=%async_computation.5 | async-start | bytes 8388608
  121.3 18.0 %slice-start.2 = ((s8[16777216]{0:T(1024)(128)(4,1)}), s8[4194304]{0:T(1024)(128)(4,1)S(1)}, s32[]{:S(2)}) async-start(s8[16777216]{0:T(1024)(128)(4,1)} %bitcast.29), calls=%async_computation.6 | async-start | bytes 8388608
  121.3 18.0 %slice-start.3 = ((s8[16777216]{0:T(1024)(128)(4,1)}), s8[4194304]{0:T(1024)(128)(4,1)S(1)}, s32[]{:S(2)}) async-start(s8[16777216]{0:T(1024)(128)(4,1)} %bitcast.29), calls=%async_computation.7 | async-start | bytes 8388608
  235.1 471.2 %reduce-scatter.2.cloned.1.call-start = ((), (), s32[]{:S(2)}) async-start(), calls=%async_computation.2 | async-start | bytes 2162688 | tf_op jit(solution)/shard_map/reduce_scatter | solution.py:94
  549.6 10.1 %copy-start = (bf16[1,2048,512]{1,2,0:T(8,128)(2,1)S(1)}, bf16[1,2048,512]{1,2,0:T(8,128)(2,1)}, u32[]{:S(2)}) copy-start(bf16[1,2048,512]{1,2,0:T(8,128)(2,1)} %copy.23) | copy-start | bytes 6291460
  559.7 146.6 %copy-start.1 = (s32[16]{0:T(128)S(1)}, s32[16]{0:T(128)}, u32[]{:S(2)}) copy-start(s32[16]{0:T(128)} %param.7) | copy-start | bytes 196
Sparse Core Ops, SparseCore 0:
  10.0 56.9 all-gather.3
  235.2 289.7 all-gather.5
  569.8 136.4 reduce-scatter.1
